TPU v7x, 32 devices: a whole 2x2x4 slice. The times are simulated.
32 devices in a mesh: prow: 8 (over z, core), pcol: 4 (over y, x).
Axes of the slice: x: 2, y: 2, z: 4, core: 2. Of those that a mesh axis runs over, the one named last changes fastest.
Arguments:
- leaf_source: bfloat16 [8, 4, 8, 256, 128], P('prow', 'pcol'), may hold values from -6 to 6
- band_source: bfloat16 [8, 256, 128], P('prow'), may hold values from -6 to 6
- strip_source: bfloat16 [4, 256, 128], P('pcol'), may hold values from -6 to 6
- summit_source: bfloat16 [256, 128], replicated, may hold values from -6 to 6
- leaf_inverse: bfloat16 [8, 4, 8, 256, 256], P('prow', 'pcol'), may hold values from -1 to 2
- band_inverse: bfloat16 [8, 256, 256], P('prow'), may hold values from -1 to 2
- strip_inverse: bfloat16 [4, 256, 256], P('pcol'), may hold values from -1 to 2
- summit_inverse: bfloat16 [256, 256], replicated, may hold values from -1 to 2
- leaf_blocks: bfloat16 [8, 4, 28, 256, 256], P('prow', 'pcol'), may hold values from -0.09375 to 0.09375
- band_blocks: bfloat16 [8, 4, 8, 256, 256], P('prow', 'pcol'), may hold values from -0.046875 to 0.046875
- strip_blocks: bfloat16 [8, 4, 8, 256, 256], P('prow', 'pcol'), may hold values from -0.03125 to 0.03125
- summit_blocks: bfloat16 [8, 4, 8, 256, 256], P('prow', 'pcol'), may hold values from -0.046875 to 0.046875
- coupling: bfloat16 [8, 4, 256, 256], P('prow', 'pcol'), may hold values from -0.09375 to 0.09375
- summit_band: bfloat16 [8, 256, 256], P('prow', 'pcol'), may hold values from -0.078125 to 0.078125
- summit_strip: bfloat16 [4, 256, 256], P('pcol'), may hold values from -0.078125 to 0.078125
- parents: int32 [8, 4, 8], P('prow', 'pcol'), may hold values from 1 to 8, as said below
- widths: int32 [8, 4, 8], P('prow', 'pcol'), may hold values from 64 to 256
Outputs:
- leaf_answer: bfloat16 [8, 4, 8, 256, 128], P('prow', 'pcol')
- band_answer: bfloat16 [8, 256, 128], P('prow')
- strip_answer: bfloat16 [4, 256, 128], P('pcol')
- summit_answer: bfloat16 [256, 128], replicated
Inputs may be any that keep to these rules, and one draw needn't show every extreme that they name: parents[r, c, a] is a later leaf of the same subtree, or 8 where leaf a links only to the separators.
All inputs are finite; a program needn't handle non-finite values.
Results may differ from a plain program's by a relative error of at most 0.015.
Values sent between devices are 32-bit elements; how exact they have to be, the bound alone decides.
No kernel may reach another device: no remote copies, remote signals or barrier semaphores. Data moves between devices by JAX's collectives and lax.ppermute only.
A program may use at most 64 MiB of HBM per device.

v0:
```python
import jax
import jax.numpy as jnp
from jax import lax
from jax.sharding import PartitionSpec as P

PASSES = 2


def ancestors(parent_list, leaf_count):
    node_ids = jnp.arange(leaf_count + 1, dtype=jnp.int32)
    current = parent_list
    extended = jnp.concatenate([current, jnp.full((1,), leaf_count, jnp.int32)])
    reached = jnp.zeros((leaf_count + 1, leaf_count), jnp.float32)
    for repeat in range(leaf_count):
        matches = current[None, :] == node_ids[:, None]
        reached = jnp.maximum(reached, matches.astype(jnp.float32))
        current = jnp.sum(jnp.where(matches, extended[:, None], 0), axis=0)
    return reached[:leaf_count]


def multiply(left, right, form):
    return jnp.einsum(form, left, right, preferred_element_type=jnp.float32)


def forward_block(inverse, source, partial_value):
    residual = (source.astype(jnp.float32) - partial_value).astype(jnp.bfloat16)
    return multiply(inverse, residual, "ij,jr->ir").astype(jnp.bfloat16)


def backward_block(inverse, source, partial_value):
    residual = (source.astype(jnp.float32) - partial_value).astype(jnp.bfloat16)
    return multiply(inverse, residual, "ji,jr->ir").astype(jnp.bfloat16)


def leaf_forward(pair_blocks, inverses, sources, reached, row_mask):
    leaf_count = sources.shape[0]
    solved = []
    for position in range(leaf_count):
        residual = sources[position].astype(jnp.float32)
        if position > 0:
            first_pair = position * (position - 1) // 2
            weights = reached[position, :position].astype(jnp.bfloat16)
            stacked = jnp.stack(solved) * weights[:, None, None]
            residual = residual - multiply(
                pair_blocks[first_pair : first_pair + position], stacked, "bij,bjr->ir"
            )
        residual = (row_mask[position] * residual).astype(jnp.bfloat16)
        solved.append(
            (row_mask[position] * multiply(inverses[position], residual, "ij,jr->ir")).astype(
                jnp.bfloat16
            )
        )
    return jnp.stack(solved)


def leaf_backward(pair_blocks, inverses, solved, outer, reached, row_mask):
    leaf_count = solved.shape[0]
    pending = outer
    answers = [None] * leaf_count
    for position in reversed(range(leaf_count)):
        residual = (
            row_mask[position] * (solved[position].astype(jnp.float32) - pending[position])
        ).astype(jnp.bfloat16)
        update = (row_mask[position] * multiply(inverses[position], residual, "ji,jr->ir")).astype(
            jnp.bfloat16
        )
        answers[position] = update
        if position > 0:
            first_pair = position * (position - 1) // 2
            pushed = multiply(
                pair_blocks[first_pair : first_pair + position], update, "bji,jr->bir"
            )
            pending = pending.at[:position].add(
                reached[position, :position][:, None, None] * pushed
            )
    return jnp.stack(answers)


def per_device(
    leaf_source,
    band_source,
    strip_source,
    summit_source,
    leaf_inverse,
    band_inverse,
    strip_inverse,
    summit_inverse,
    leaf_blocks,
    band_blocks,
    strip_blocks,
    summit_blocks,
    coupling,
    summit_band,
    summit_strip,
    parents,
    widths,
):
    leaf_count = leaf_source.shape[2]
    block_width = leaf_source.shape[3]
    reached = ancestors(parents[0, 0], leaf_count)
    column_ids = jnp.arange(block_width, dtype=jnp.int32)
    row_mask = (column_ids[None, :] < widths[0, 0][:, None]).astype(jnp.float32)[:, :, None]
    band_slab = summit_band.shape[1]
    column_place = lax.axis_index("pcol") * band_slab
    inverses = leaf_inverse[0, 0]
    pair_blocks = leaf_blocks[0, 0]
    to_band = band_blocks[0, 0]
    to_strip = strip_blocks[0, 0]
    to_summit = summit_blocks[0, 0]
    link_block = coupling[0, 0]
    lift_band = summit_band[0]
    lift_strip = summit_strip[0]
    current = (leaf_source[0, 0], band_source[0], strip_source[0], summit_source)
    for iteration in range(PASSES):
        leaf_now, band_now, strip_now, summit_now = current
        solved = leaf_forward(pair_blocks, inverses, leaf_now, reached, row_mask)
        band_term = multiply(to_band, solved, "aij,ajr->ir")
        strip_term = multiply(to_strip, solved, "aij,ajr->ir")
        summit_term = multiply(to_summit, solved, "aij,ajr->ir")
        band_partial = lax.psum(band_term, "pcol")
        band_solved = forward_block(band_inverse[0], band_now, band_partial)
        own_band = lax.dynamic_slice_in_dim(band_solved, column_place, band_slab, 0)
        summit_term = summit_term + multiply(lift_band, own_band, "ki,kn->in")
        strip_term = strip_term + multiply(link_block, band_solved, "ij,jn->in")
        strip_partial, summit_early = lax.psum((strip_term, summit_term), "prow")
        strip_solved = forward_block(strip_inverse[0], strip_now, strip_partial)
        summit_partial = lax.psum(
            summit_early + multiply(lift_strip, strip_solved, "ki,kn->in"), "pcol"
        )
        summit_solved = forward_block(summit_inverse, summit_now, summit_partial)
        summit_answer = backward_block(
            summit_inverse, summit_solved, jnp.zeros(summit_solved.shape, jnp.float32)
        )
        strip_answer = backward_block(
            strip_inverse[0], strip_solved, multiply(lift_strip, summit_answer, "ki,in->kn")
        )
        downward = multiply(link_block, strip_answer, "ji,jn->in")
        band_piece = multiply(lift_band, summit_answer, "ki,in->kn")
        band_back = lax.psum(downward, "pcol") + lax.all_gather(
            band_piece, "pcol", axis=0, tiled=True
        )
        band_answer = backward_block(band_inverse[0], band_solved, band_back)
        outer = (
            multiply(to_band, band_answer, "aij,ir->ajr")
            + multiply(to_strip, strip_answer, "aij,ir->ajr")
            + multiply(to_summit, summit_answer, "aij,ir->ajr")
        )
        leaf_answer = leaf_backward(pair_blocks, inverses, solved, outer, reached, row_mask)
        current = (leaf_answer, band_answer, strip_answer, summit_answer)
    return (current[0][None, None], current[1][None], current[2][None], current[3])


def solution(mesh):
    placed = (
        P("prow", "pcol", None, None, None),
        P("prow", None, None),
        P("pcol", None, None),
        P(),
        P("prow", "pcol", None, None, None),
        P("prow", None, None),
        P("pcol", None, None),
        P(),
        P("prow", "pcol", None, None, None),
        P("prow", "pcol", None, None, None),
        P("prow", "pcol", None, None, None),
        P("prow", "pcol", None, None, None),
        P("prow", "pcol", None, None),
        P("prow", "pcol", None),
        P("pcol", None, None),
        P("prow", "pcol", None),
        P("prow", "pcol", None),
    )
    return jax.shard_map(
        per_device,
        mesh=mesh,
        in_specs=placed,
        out_specs=(
            P("prow", "pcol", None, None, None),
            P("prow", None, None),
            P("pcol", None, None),
            P(),
        ),
        check_vma=False,
    )
```

profile of v0, /device:TPU:0, one launch (start us, length us, event | category | flops | bytes accessed | tf_op | source)
XLA Modules:
  0.0 482.1 jit_solution(6182447190945887679)
XLA Ops:
  21.9 2.2 constant_dynamic-update-slice_fusion.13
  25.1 2.5 constant_dynamic-update-slice_fusion.12
  28.4 2.6 constant_dynamic-update-slice_fusion.11
  31.0 2.6 constant_dynamic-update-slice_fusion.18
  33.6 2.2 convolution_bitcast_fusion.21
  45.1 35.8 %all-reduce.11.cloned.1.call-done = f32[256,128]{1,0:T(8,128)} async-done(((f32[256,128]{1,0:T(8,128)}), f32[256,128]{1,0:T(8,128)}) %all-reduce.11.cloned.1.call-update) | async-done | bytes 131088 | tf_op jit(solution)/shard_map/psum | solution.py:120
  87.1 54.4 %all-reduce.25.cloned.1.call-done = (f32[256,128]{1,0:T(8,128)}, f32[256,128]{1,0:T(8,128)}) async-done(((f32[256,128]{1,0:T(8,128)}, f32[256,128]{1,0:T(8,128)}), (f32[256,128]{1,0:T(8,128)}, f32[256,128]{1,0:T(8,128)})) %all-reduce.25.cloned.1.call-update) | async-done | bytes 262160 | tf_op jit(solution)/shard_map/psum | solution.py:125
  146.3 40.2 %all-reduce.13.cloned.1.call-done = f32[256,128]{1,0:T(8,128)} async-done(((f32[256,128]{1,0:T(8,128)}), f32[256,128]{1,0:T(8,128)}) %all-reduce.13.cloned.1.call-update) | async-done | bytes 131088 | tf_op jit(solution)/shard_map/psum | solution.py:127
  193.0 9.1 %all_gather.6 = f32[256,128]{1,0:T(8,128)} all-gather(f32[64,128]{1,0:T(8,128)S(1)} %convolution_bitcast_fusion.24), channel_id=1, replica_groups=mesh['prow'=8,'pcol'=4] {'pcol'}, dimensions={0}, use_global_device_ids=true | all-gather | bytes 163840 | tf_op jit(solution)/shard_map/all_gather | solution.py:139
  203.8 30.6 %all-reduce.15.cloned.1.call-done = f32[256,128]{0,1:T(8,128)} async-done(((f32[256,128]{0,1:T(8,128)}), f32[256,128]{0,1:T(8,128)}) %all-reduce.15.cloned.1.call-update) | async-done | bytes 131088 | tf_op jit(solution)/shard_map/psum | solution.py:139
  248.7 2.2 constant_dynamic-update-slice_fusion.41
  250.9 2.3 constant_dynamic-update-slice_fusion.40
  253.2 2.4 constant_dynamic-update-slice_fusion.39
  255.6 2.5 constant_dynamic-update-slice_fusion.38
  258.1 2.6 constant_dynamic-update-slice_fusion.37
  260.7 2.7 constant_dynamic-update-slice_fusion.44
  263.4 2.2 convolution_bitcast_fusion.15
  265.6 2.2 convolution_bitcast_fusion.17
  267.9 2.2 convolution_bitcast_fusion.16
  270.0 40.1 %all-reduce.17.cloned.1.call-done = f32[256,128]{0,1:T(8,128)} async-done(((f32[256,128]{0,1:T(8,128)}), f32[256,128]{0,1:T(8,128)}) %all-reduce.17.cloned.1.call-update) | async-done | bytes 131088 | tf_op jit(solution)/shard_map/psum | solution.py:120
  315.1 55.6 %all-reduce.23.cloned.1.call-done = (f32[256,128]{0,1:T(8,128)}, f32[256,128]{0,1:T(8,128)}) async-done(((f32[256,128]{0,1:T(8,128)}, f32[256,128]{0,1:T(8,128)}), (f32[256,128]{0,1:T(8,128)}, f32[256,128]{0,1:T(8,128)})) %all-reduce.23.cloned.1.call-update) | async-done | bytes 262160 | tf_op jit(solution)/shard_map/psum | solution.py:125
  374.2 41.4 %all-reduce.19.cloned.1.call-done = f32[256,128]{0,1:T(8,128)} async-done(((f32[256,128]{0,1:T(8,128)}), f32[256,128]{0,1:T(8,128)}) %all-reduce.19.cloned.1.call-update) | async-done | bytes 131088 | tf_op jit(solution)/shard_map/psum | solution.py:127
  425.4 8.8 %all_gather.7 = f32[256,128]{1,0:T(8,128)S(1)} all-gather(f32[64,128]{1,0:T(8,128)S(1)} %convolution_bitcast_fusion.23), channel_id=1, replica_groups=mesh['prow'=8,'pcol'=4] {'pcol'}, dimensions={0}, use_global_device_ids=true | all-gather | bytes 163840 | tf_op jit(solution)/shard_map/all_gather | solution.py:139
  434.2 29.4 %all-reduce.21.cloned.1.call-done = f32[256,128]{0,1:T(8,128)} async-done(((f32[256,128]{0,1:T(8,128)}), f32[256,128]{0,1:T(8,128)}) %all-reduce.21.cloned.1.call-update) | async-done | bytes 131088 | tf_op jit(solution)/shard_map/psum | solution.py:139
  (281 shorter events, 87.4 us)
Async XLA Ops:
  7.2 26.5 %copy-start = (bf16[1,1,8,256,256]{4,3,2,1,0:T(8,128)(2,1)S(1)}, bf16[1,1,8,256,256]{4,3,2,1,0:T(8,128)(2,1)}, u32[]{:S(2)}) copy-start(bf16[1,1,8,256,256]{4,3,2,1,0:T(8,128)(2,1)} %param.54) | copy-start | bytes 3145732
  7.2 73.7 %all-reduce.11.cloned.1.call-start = ((), (), s32[]{:S(2)}) async-start(), calls=%async_computation | async-start | bytes 262144 | tf_op jit(solution)/shard_map/psum | solution.py:120
  10.5 20.5 %copy-start.73 = (bf16[7]{0:T(256)(128)(2,1)}, bf16[7]{0:T(256)(128)(2,1)S(1)}, u32[]{:S(2)}) copy-start(bf16[7]{0:T(256)(128)(2,1)S(1)} %fusion.586) | copy-start | bytes 46
  10.5 17.8 %copy-start.74 = (bf16[6]{0:T(256)(128)(2,1)}, bf16[6]{0:T(256)(128)(2,1)S(1)}, u32[]{:S(2)}) copy-start(bf16[6]{0:T(256)(128)(2,1)S(1)} %fusion.585) | copy-start | bytes 40
  10.6 14.5 %copy-start.75 = (bf16[5]{0:T(256)(128)(2,1)}, bf16[5]{0:T(256)(128)(2,1)S(1)}, u32[]{:S(2)}) copy-start(bf16[5]{0:T(256)(128)(2,1)S(1)} %fusion.584) | copy-start | bytes 34
  10.6 13.6 %copy-start.76 = (bf16[4]{0:T(256)(128)(2,1)}, bf16[4]{0:T(256)(128)(2,1)S(1)}, u32[]{:S(2)}) copy-start(bf16[4]{0:T(256)(128)(2,1)S(1)} %fusion.583) | copy-start | bytes 28
  10.6 13.5 %copy-start.77 = (bf16[3]{0:T(256)(128)(2,1)}, bf16[3]{0:T(256)(128)(2,1)S(1)}, u32[]{:S(2)}) copy-start(bf16[3]{0:T(256)(128)(2,1)S(1)} %fusion.582) | copy-start | bytes 22
  10.6 13.5 %copy-start.78 = (bf16[2]{0:T(256)(128)(2,1)}, bf16[2]{0:T(256)(128)(2,1)S(1)}, u32[]{:S(2)}) copy-start(bf16[2]{0:T(256)(128)(2,1)S(1)} %fusion.581) | copy-start | bytes 16
  12.1 16.3 %copy-start.48 = (f32[1,256]{1,0:T(1,128)}, f32[1,256]{1,0:T(1,128)S(1)}, u32[]{:S(2)}) copy-start(f32[1,256]{1,0:T(1,128)S(1)} %get-tuple-element.242) | copy-start | bytes 3076
  12.1 18.9 %copy-start.51 = (f32[1,256]{1,0:T(1,128)}, f32[1,256]{1,0:T(1,128)S(1)}, u32[]{:S(2)}) copy-start(f32[1,256]{1,0:T(1,128)S(1)} %get-tuple-element.241) | copy-start | bytes 3076
  25.1 15.7 %copy-start.2 = (bf16[1,1,8,256,256]{4,3,2,1,0:T(8,128)(2,1)S(1)}, bf16[1,1,8,256,256]{4,3,2,1,0:T(8,128)(2,1)}, u32[]{:S(2)}) copy-start(bf16[1,1,8,256,256]{4,3,2,1,0:T(8,128)(2,1)} %param.56) | copy-start | bytes 3145732
  28.4 14.6 %copy-start.1 = (bf16[1,1,8,256,256]{4,3,2,1,0:T(8,128)(2,1)S(1)}, bf16[1,1,8,256,256]{4,3,2,1,0:T(8,128)(2,1)}, u32[]{:S(2)}) copy-start(bf16[1,1,8,256,256]{4,3,2,1,0:T(8,128)(2,1)} %param.55) | copy-start | bytes 3145732
  31.0 51.1 %copy-start.10 = (bf16[1,1,256,256]{3,2,1,0:T(8,128)(2,1)S(1)}, bf16[1,1,256,256]{3,2,1,0:T(8,128)(2,1)}, u32[]{:S(2)}) copy-start(bf16[1,1,256,256]{3,2,1,0:T(8,128)(2,1)} %param.57) | copy-start | bytes 393220
  33.6 107.8 %copy-start.8 = (bf16[1,256,256]{2,1,0:T(8,128)(2,1)S(1)}, bf16[1,256,256]{2,1,0:T(8,128)(2,1)}, u32[]{:S(2)}) copy-start(bf16[1,256,256]{2,1,0:T(8,128)(2,1)} %param.51) | copy-start | bytes 393220
  33.6 109.6 %copy-start.9 = (bf16[1,256,256]{2,1,0:T(8,128)(2,1)S(1)}, bf16[1,256,256]{2,1,0:T(8,128)(2,1)}, u32[]{:S(2)}) copy-start(bf16[1,256,256]{2,1,0:T(8,128)(2,1)} %param.59) | copy-start | bytes 393220
  35.8 105.6 %all-reduce.25.cloned.1.call-start = ((), (), s32[]{:S(2)}) async-start(), calls=%async_computation.7 | async-start | bytes 524288 | tf_op jit(solution)/shard_map/psum | solution.py:125
  85.8 100.7 %all-reduce.13.cloned.1.call-start = ((), (), s32[]{:S(2)}) async-start(), calls=%async_computation.1 | async-start | bytes 262144 | tf_op jit(solution)/shard_map/psum | solution.py:127
  145.0 89.3 %all-reduce.15.cloned.1.call-start = ((), (), s32[]{:S(2)}) async-start(), calls=%async_computation.2 | async-start | bytes 262144 | tf_op jit(solution)/shard_map/psum | solution.py:139
  192.0 118.2 %all-reduce.17.cloned.1.call-start = ((), (), s32[]{:S(2)}) async-start(), calls=%async_computation.3 | async-start | bytes 262144 | tf_op jit(solution)/shard_map/psum | solution.py:120
  267.8 102.9 %all-reduce.23.cloned.1.call-start = ((), (), s32[]{:S(2)}) async-start(), calls=%async_computation.6 | async-start | bytes 524288 | tf_op jit(solution)/shard_map/psum | solution.py:125
  315.0 100.6 %all-reduce.19.cloned.1.call-start = ((), (), s32[]{:S(2)}) async-start(), calls=%async_computation.4 | async-start | bytes 262144 | tf_op jit(solution)/shard_map/psum | solution.py:127
  374.2 89.4 %all-reduce.21.cloned.1.call-start = ((), (), s32[]{:S(2)}) async-start(), calls=%async_computation.5 | async-start | bytes 262144 | tf_op jit(solution)/shard_map/psum | solution.py:139
  419.5 47.3 %copy-start.13 = (bf16[128,256]{1,0:T(8,128)(2,1)S(1)}, bf16[128,256]{1,0:T(8,128)(2,1)}, u32[]{:S(2)}) copy-start(bf16[128,256]{1,0:T(8,128)(2,1)} %convolution_convert_fusion.1) | copy-start | bytes 196612
  419.5 49.0 %copy-start.11 = (bf16[128,256]{1,0:T(8,128)(2,1)S(1)}, bf16[128,256]{1,0:T(8,128)(2,1)}, u32[]{:S(2)}) copy-start(bf16[128,256]{1,0:T(8,128)(2,1)} %convolution_convert_fusion.2) | copy-start | bytes 196612
  (63 other events, 156.5 us)
Sparse Core Ops, SparseCore 0:
  36.0 44.9 all-reduce.10
  85.9 55.5 all-reduce.24
  145.1 41.2 all-reduce.12
  192.1 42.2 all-reduce.14
  267.9 42.2 all-reduce.16
  315.1 55.5 all-reduce.22
  374.3 41.2 all-reduce.18
  421.3 42.2 all-reduce.20
where the time goes:
time: 484 us; the launch traced here: 482 us
  waiting for transfers between devices  328 us (68%)
  matrix products  94.3 us (19%)
  local copies, waits for them, and re-layouts  22.6 us (5%)
  blocking collectives  17.8 us (4%)
  between operations  16 us (3%)
    psum x2, waiting for transfers between devices, per_device(): strip_partial, summit_early = lax.psum((strip_term, summit_term), 'prow')  110 us
    dot_general x76, matrix products, multiply(): return jnp.einsum(form, left, right, preferred_element_type=jnp.float32)  94.3 us
    psum x2, waiting for transfers between devices, per_device(): lax.psum(summit_early + multiply(lift_strip, strip_solved, 'ki,kn->in'),...  81.6 us
    psum x2, waiting for transfers between devices, per_device(): band_partial = lax.psum(band_term, 'pcol')  76 us
    psum x2, waiting for transfers between devices, per_device(): lax.psum(downward, 'pcol')  60 us
    all_gather x2, blocking collectives, per_device(): lax.all_gather(band_piece, 'pcol', axis=0, tiled=True)  17.8 us
    unnamed x175, local copies, waits for them, and re-layouts  11.7 us
  transfers between devices with their start and end apart: 8, of which 8 were waited for; matrix products, arithmetic and copies ran while one was open for 4% of the time, Pallas kernels for 0%

commit v1 on v0

--- a/solution.py
+++ b/solution.py
@@ -136,7 +136,7 @@
         )
         downward = multiply(link_block, strip_answer, "ji,jn->in")
         band_piece = multiply(lift_band, summit_answer, "ki,in->kn")
-        band_back = lax.psum(downward, "pcol") + lax.all_gather(
+        band_back = jnp.sum(lax.all_gather(downward, "pcol"), axis=0) + lax.all_gather(
             band_piece, "pcol", axis=0, tiled=True
         )
         band_answer = backward_block(band_inverse[0], band_solved, band_back)

time: 484 us -> 452 us (0.934)
  waiting for transfers between devices: 328 us -> 268 us
  blocking collectives: 17.8 us -> 38.8 us
    psum x2 -> x0, waiting for transfers between devices: 60 us -> none  [per_device(): lax.psum(downward, 'pcol')]
    all_gather x0 -> x2, blocking collectives: none -> 21 us  [per_device(): lax.all_gather(downward, 'pcol')]
  transfers between devices with their start and end apart: 8 -> 6, of which waited for: 8 -> 6; matrix products, arithmetic and copies ran while one was open for 4% -> 3% of each run, Pallas kernels for 0% -> 0%
where the time goes in v1:
time: 452 us; the launch traced here: 450 us
  waiting for transfers between devices  268 us (59%)
  matrix products  92.7 us (21%)
  blocking collectives  38.8 us (9%)
  local copies, waits for them, and re-layouts  27.3 us (6%)
  between operations  15.9 us (4%)
  other arithmetic  6.84 us (2%)
    psum x2, waiting for transfers between devices, per_device(): strip_partial, summit_early = lax.psum((strip_term, summit_term), 'prow')  110 us
    dot_general x76, matrix products, multiply(): return jnp.einsum(form, left, right, preferred_element_type=jnp.float32)  92.7 us
    psum x2, waiting for transfers between devices, per_device(): lax.psum(summit_early + multiply(lift_strip, strip_solved, 'ki,kn->in'),...  81.6 us
    psum x2, waiting for transfers between devices, per_device(): band_partial = lax.psum(band_term, 'pcol')  76.1 us
    all_gather x2, blocking collectives, per_device(): lax.all_gather(downward, 'pcol')  21 us
    all_gather x2, blocking collectives, per_device(): lax.all_gather(band_piece, 'pcol', axis=0, tiled=True)  17.8 us
    unnamed x175, local copies, waits for them, and re-layouts  11.8 us
  transfers between devices with their start and end apart: 6, of which 6 were waited for; matrix products, arithmetic and copies ran while one was open for 3% of the time, Pallas kernels for 0%

profile of v1, /device:TPU:0, one launch (start us, length us, event | category | flops | bytes accessed | tf_op | source)
XLA Modules:
  0.0 449.6 jit_solution(3051293058543261053)
XLA Ops:
  21.8 2.2 constant_dynamic-update-slice_fusion.13
  25.1 2.5 constant_dynamic-update-slice_fusion.12
  28.4 2.6 constant_dynamic-update-slice_fusion.11
  31.0 2.6 constant_dynamic-update-slice_fusion.18
  33.6 2.2 convolution_bitcast_fusion.21
  44.9 36.0 %all-reduce.9.cloned.1.call-done = f32[256,128]{1,0:T(8,128)} async-done(((f32[256,128]{1,0:T(8,128)}), f32[256,128]{1,0:T(8,128)}) %all-reduce.9.cloned.1.call-update) | async-done | bytes 131088 | tf_op jit(solution)/shard_map/psum | solution.py:120
  87.1 54.4 %all-reduce.19.cloned.1.call-done = (f32[256,128]{1,0:T(8,128)}, f32[256,128]{1,0:T(8,128)}) async-done(((f32[256,128]{1,0:T(8,128)}, f32[256,128]{1,0:T(8,128)}), (f32[256,128]{1,0:T(8,128)}, f32[256,128]{1,0:T(8,128)})) %all-reduce.19.cloned.1.call-update) | async-done | bytes 262160 | tf_op jit(solution)/shard_map/psum | solution.py:125
  146.3 40.2 %all-reduce.11.cloned.1.call-done = f32[256,128]{1,0:T(8,128)} async-done(((f32[256,128]{1,0:T(8,128)}), f32[256,128]{1,0:T(8,128)}) %all-reduce.11.cloned.1.call-update) | async-done | bytes 131088 | tf_op jit(solution)/shard_map/psum | solution.py:127
  191.2 9.1 %all_gather.20 = f32[256,128]{1,0:T(8,128)} all-gather(f32[64,128]{1,0:T(8,128)S(1)} %convolution_bitcast_fusion.24), channel_id=1, replica_groups=mesh['prow'=8,'pcol'=4] {'pcol'}, dimensions={0}, use_global_device_ids=true | all-gather | bytes 163840 | tf_op jit(solution)/shard_map/all_gather | solution.py:139
  203.0 10.5 %all-gather = f32[1024,128]{0,1:T(8,128)} all-gather(f32[256,128]{0,1:T(8,128)S(1)} %convolution_bitcast_fusion.11), channel_id=2, replica_groups=mesh['prow'=8,'pcol'=4] {'pcol'}, dimensions={0}, use_global_device_ids=true | all-gather | bytes 655360 | tf_op jit(solution)/shard_map/all_gather | solution.py:139
  231.8 2.2 constant_dynamic-update-slice_fusion.41
  234.0 2.3 constant_dynamic-update-slice_fusion.40
  236.3 2.4 constant_dynamic-update-slice_fusion.39
  238.7 2.5 constant_dynamic-update-slice_fusion.38
  241.2 2.6 constant_dynamic-update-slice_fusion.37
  243.8 2.7 constant_dynamic-update-slice_fusion.44
  246.5 2.2 convolution_bitcast_fusion.15
  248.7 2.2 convolution_bitcast_fusion.17
  250.9 2.2 convolution_bitcast_fusion.16
  253.1 40.1 %all-reduce.13.cloned.1.call-done = f32[256,128]{0,1:T(8,128)} async-done(((f32[256,128]{0,1:T(8,128)}), f32[256,128]{0,1:T(8,128)}) %all-reduce.13.cloned.1.call-update) | async-done | bytes 131088 | tf_op jit(solution)/shard_map/psum | solution.py:120
  298.1 55.6 %all-reduce.17.cloned.1.call-done = (f32[256,128]{0,1:T(8,128)}, f32[256,128]{0,1:T(8,128)}) async-done(((f32[256,128]{0,1:T(8,128)}, f32[256,128]{0,1:T(8,128)}), (f32[256,128]{0,1:T(8,128)}, f32[256,128]{0,1:T(8,128)})) %all-reduce.17.cloned.1.call-update) | async-done | bytes 262160 | tf_op jit(solution)/shard_map/psum | solution.py:125
  357.2 41.4 %all-reduce.15.cloned.1.call-done = f32[256,128]{0,1:T(8,128)} async-done(((f32[256,128]{0,1:T(8,128)}), f32[256,128]{0,1:T(8,128)}) %all-reduce.15.cloned.1.call-update) | async-done | bytes 131088 | tf_op jit(solution)/shard_map/psum | solution.py:127
  407.7 8.8 %all_gather.23 = f32[256,128]{1,0:T(8,128)S(1)} all-gather(f32[64,128]{1,0:T(8,128)S(1)} %convolution_bitcast_fusion.23), channel_id=1, replica_groups=mesh['prow'=8,'pcol'=4] {'pcol'}, dimensions={0}, use_global_device_ids=true | all-gather | bytes 163840 | tf_op jit(solution)/shard_map/all_gather | solution.py:139
  417.2 10.5 %all-gather.1 = f32[1024,128]{0,1:T(8,128)} all-gather(f32[256,128]{0,1:T(8,128)S(1)} %convolution_bitcast_fusion.8), channel_id=3, replica_groups=mesh['prow'=8,'pcol'=4] {'pcol'}, dimensions={0}, use_global_device_ids=true | all-gather | bytes 655360 | tf_op jit(solution)/shard_map/all_gather | solution.py:139
  (281 shorter events, 93.8 us)
Async XLA Ops:
  7.2 26.4 %copy-start = (bf16[1,1,8,256,256]{4,3,2,1,0:T(8,128)(2,1)S(1)}, bf16[1,1,8,256,256]{4,3,2,1,0:T(8,128)(2,1)}, u32[]{:S(2)}) copy-start(bf16[1,1,8,256,256]{4,3,2,1,0:T(8,128)(2,1)} %param.54) | copy-start | bytes 3145732
  7.2 73.7 %all-reduce.9.cloned.1.call-start = ((), (), s32[]{:S(2)}) async-start(), calls=%async_computation | async-start | bytes 262144 | tf_op jit(solution)/shard_map/psum | solution.py:120
  10.5 20.4 %copy-start.73 = (bf16[7]{0:T(256)(128)(2,1)}, bf16[7]{0:T(256)(128)(2,1)S(1)}, u32[]{:S(2)}) copy-start(bf16[7]{0:T(256)(128)(2,1)S(1)} %fusion.586) | copy-start | bytes 46
  10.5 17.8 %copy-start.74 = (bf16[6]{0:T(256)(128)(2,1)}, bf16[6]{0:T(256)(128)(2,1)S(1)}, u32[]{:S(2)}) copy-start(bf16[6]{0:T(256)(128)(2,1)S(1)} %fusion.585) | copy-start | bytes 40
  10.5 14.5 %copy-start.75 = (bf16[5]{0:T(256)(128)(2,1)}, bf16[5]{0:T(256)(128)(2,1)S(1)}, u32[]{:S(2)}) copy-start(bf16[5]{0:T(256)(128)(2,1)S(1)} %fusion.584) | copy-start | bytes 34
  10.6 13.5 %copy-start.76 = (bf16[4]{0:T(256)(128)(2,1)}, bf16[4]{0:T(256)(128)(2,1)S(1)}, u32[]{:S(2)}) copy-start(bf16[4]{0:T(256)(128)(2,1)S(1)} %fusion.583) | copy-start | bytes 28
  10.6 13.5 %copy-start.77 = (bf16[3]{0:T(256)(128)(2,1)}, bf16[3]{0:T(256)(128)(2,1)S(1)}, u32[]{:S(2)}) copy-start(bf16[3]{0:T(256)(128)(2,1)S(1)} %fusion.582) | copy-start | bytes 22
  10.6 13.4 %copy-start.78 = (bf16[2]{0:T(256)(128)(2,1)}, bf16[2]{0:T(256)(128)(2,1)S(1)}, u32[]{:S(2)}) copy-start(bf16[2]{0:T(256)(128)(2,1)S(1)} %fusion.581) | copy-start | bytes 16
  11.9 12.1 %copy-start.55 = (f32[1,256]{1,0:T(1,128)}, f32[1,256]{1,0:T(1,128)S(1)}, u32[]{:S(2)}) copy-start(f32[1,256]{1,0:T(1,128)S(1)} %get-tuple-element.248) | copy-start | bytes 3076
  11.9 13.1 %copy-start.45 = (f32[1,256]{1,0:T(1,128)}, f32[1,256]{1,0:T(1,128)S(1)}, u32[]{:S(2)}) copy-start(f32[1,256]{1,0:T(1,128)S(1)} %get-tuple-element.243) | copy-start | bytes 3076
  12.0 16.4 %copy-start.48 = (f32[1,256]{1,0:T(1,128)}, f32[1,256]{1,0:T(1,128)S(1)}, u32[]{:S(2)}) copy-start(f32[1,256]{1,0:T(1,128)S(1)} %get-tuple-element.242) | copy-start | bytes 3076
  12.0 19.0 %copy-start.51 = (f32[1,256]{1,0:T(1,128)}, f32[1,256]{1,0:T(1,128)S(1)}, u32[]{:S(2)}) copy-start(f32[1,256]{1,0:T(1,128)S(1)} %get-tuple-element.241) | copy-start | bytes 3076
  15.7 11.8 %copy-start.26 = (bf16[128,256]{1,0:T(8,128)(2,1)}, bf16[128,256]{1,0:T(8,128)(2,1)S(1)}, u32[]{:S(2)}) copy-start(bf16[128,256]{1,0:T(8,128)(2,1)S(1)} %get-tuple-element.249) | copy-start | bytes 196612
  25.1 15.6 %copy-start.2 = (bf16[1,1,8,256,256]{4,3,2,1,0:T(8,128)(2,1)S(1)}, bf16[1,1,8,256,256]{4,3,2,1,0:T(8,128)(2,1)}, u32[]{:S(2)}) copy-start(bf16[1,1,8,256,256]{4,3,2,1,0:T(8,128)(2,1)} %param.56) | copy-start | bytes 3145732
  28.4 14.5 %copy-start.1 = (bf16[1,1,8,256,256]{4,3,2,1,0:T(8,128)(2,1)S(1)}, bf16[1,1,8,256,256]{4,3,2,1,0:T(8,128)(2,1)}, u32[]{:S(2)}) copy-start(bf16[1,1,8,256,256]{4,3,2,1,0:T(8,128)(2,1)} %param.55) | copy-start | bytes 3145732
  31.0 51.1 %copy-start.10 = (bf16[1,1,256,256]{3,2,1,0:T(8,128)(2,1)S(1)}, bf16[1,1,256,256]{3,2,1,0:T(8,128)(2,1)}, u32[]{:S(2)}) copy-start(bf16[1,1,256,256]{3,2,1,0:T(8,128)(2,1)} %param.57) | copy-start | bytes 393220
  33.6 107.9 %copy-start.8 = (bf16[1,256,256]{2,1,0:T(8,128)(2,1)S(1)}, bf16[1,256,256]{2,1,0:T(8,128)(2,1)}, u32[]{:S(2)}) copy-start(bf16[1,256,256]{2,1,0:T(8,128)(2,1)} %param.51) | copy-start | bytes 393220
  33.6 109.6 %copy-start.9 = (bf16[1,256,256]{2,1,0:T(8,128)(2,1)S(1)}, bf16[1,256,256]{2,1,0:T(8,128)(2,1)}, u32[]{:S(2)}) copy-start(bf16[1,256,256]{2,1,0:T(8,128)(2,1)} %param.59) | copy-start | bytes 393220
  35.8 105.6 %all-reduce.19.cloned.1.call-start = ((), (), s32[]{:S(2)}) async-start(), calls=%async_computation.5 | async-start | bytes 524288 | tf_op jit(solution)/shard_map/psum | solution.py:125
  85.7 100.7 %all-reduce.11.cloned.1.call-start = ((), (), s32[]{:S(2)}) async-start(), calls=%async_computation.1 | async-start | bytes 262144 | tf_op jit(solution)/shard_map/psum | solution.py:127
  145.0 148.2 %all-reduce.13.cloned.1.call-start = ((), (), s32[]{:S(2)}) async-start(), calls=%async_computation.2 | async-start | bytes 262144 | tf_op jit(solution)/shard_map/psum | solution.py:120
  250.9 102.9 %all-reduce.17.cloned.1.call-start = ((), (), s32[]{:S(2)}) async-start(), calls=%async_computation.4 | async-start | bytes 524288 | tf_op jit(solution)/shard_map/psum | solution.py:125
  298.1 100.6 %all-reduce.15.cloned.1.call-start = ((), (), s32[]{:S(2)}) async-start(), calls=%async_computation.3 | async-start | bytes 262144 | tf_op jit(solution)/shard_map/psum | solution.py:127
  402.5 31.9 %copy-start.13 = (bf16[128,256]{1,0:T(8,128)(2,1)S(1)}, bf16[128,256]{1,0:T(8,128)(2,1)}, u32[]{:S(2)}) copy-start(bf16[128,256]{1,0:T(8,128)(2,1)} %convolution_convert_fusion.1) | copy-start | bytes 196612
  (61 other events, 127.8 us)
Sparse Core Ops, SparseCore 0:
  35.9 44.9 all-reduce.8
  85.9 55.5 all-reduce.18
  145.1 41.2 all-reduce.10
  251.0 42.1 all-reduce.12
  298.2 55.5 all-reduce.16
  357.4 41.2 all-reduce.14
